TPU v7x, 512 devices: a whole 4x4x16 slice. The times are simulated.
512 devices in a mesh: row: 32 (over z, core), col: 16 (over y, x).
Axes of the slice: x: 4, y: 4, z: 16, core: 2. Of those that a mesh axis runs over, the one named last changes fastest.
Arguments:
- tokens: bfloat16 [512, 16384], P('col', 'row'), may hold values from -6 to 6
- query_weight: bfloat16 [16384, 8192], P('row', 'col'), may hold values from -0.09375 to 0.09375
- keyval_weight: bfloat16 [16384, 2048], P('row', 'col'), may hold values from -0.09375 to 0.09375
Outputs:
- query_proj: bfloat16 [512, 8192], P('row', 'col')
- query_code: bfloat16 [16384, 8192], P('row', 'col')
- query_scale: float32 [128, 64], P('row', 'col')
- keyval_code: bfloat16 [16384, 2048], P('row', 'col')
- keyval_scale: float32 [128, 16], P('row', 'col')
All inputs are finite; a program needn't handle non-finite values. Where the computation divides by a largest or mean magnitude, that divisor is 1e-20 or more.
Results may differ from a plain program's by a relative error of at most 0.0095.
Values may be sent and summed in bfloat16 or wider, within the bound.
No kernel may reach another device: no remote copies, remote signals or barrier semaphores. Data moves between devices by JAX's collectives and lax.ppermute only.
A program may use at most 64 MiB of HBM per device.

v0:
```python
import math
import jax
import jax.numpy as jnp
from jax import lax
from jax.sharding import PartitionSpec as P

BLOCK = 128
QSTEPS = 4
EPSILON = 1e-06
SOFTNESS = 0.9
TWO_PI = 2.0 * math.pi


def soften(argument):
    return argument - SOFTNESS * jnp.sin(TWO_PI * argument) / TWO_PI


def block_codes(weight, smooth):
    smoothed = weight.astype(jnp.float32) * smooth[:, None]
    height, breadth = smoothed.shape
    tile_view = smoothed.reshape(height // BLOCK, BLOCK, breadth // BLOCK, BLOCK)
    scales = (jnp.max(jnp.abs(tile_view), axis=(1, 3)) + EPSILON) / QSTEPS
    encoded = (
        soften(tile_view / scales[:, None, :, None]).reshape(height, breadth).astype(jnp.bfloat16)
    )
    return (encoded, scales)


def token_encode(x_smooth, row_peak):
    token_scale = ((row_peak + EPSILON) / QSTEPS).astype(jnp.bfloat16)
    encoded = soften(x_smooth / token_scale.astype(jnp.float32)[:, None]).astype(jnp.bfloat16)
    return (encoded, token_scale)


def body(tokens, query_weight, keyval_weight):
    act_local = jnp.max(jnp.abs(tokens), axis=0).astype(jnp.float32)
    weight_local = jnp.maximum(
        jnp.max(jnp.abs(query_weight), axis=1), jnp.max(jnp.abs(keyval_weight), axis=1)
    ).astype(jnp.float32)
    act_peak, weight_peak = lax.pmax((act_local, weight_local), "col")
    smooth = jnp.sqrt((act_peak + EPSILON) / (weight_peak + EPSILON))
    query_code, query_scale = block_codes(query_weight, smooth)
    keyval_code, keyval_scale = block_codes(keyval_weight, smooth)
    x_smooth = tokens.astype(jnp.float32) / smooth[None, :]
    row_peak = lax.pmax(jnp.max(jnp.abs(x_smooth), axis=1), "row")
    local_code, local_scale = token_encode(x_smooth, row_peak)
    x_code, token_scale = (
        lax.all_gather(local_code, "col", axis=0, tiled=True),
        lax.all_gather(local_scale, "col", axis=0, tiled=True),
    )
    column_scale = jnp.repeat(query_scale, BLOCK, axis=1)
    block_total = query_code.shape[0] // BLOCK
    out_width = query_code.shape[1]
    own_rows = x_code.shape[0] // lax.axis_size("row")
    scale_rows = token_scale.astype(jnp.float32)

    def add_block(block_index, running):
        code_block = lax.dynamic_slice_in_dim(x_code, block_index * BLOCK, BLOCK, 1)
        weight_block = lax.dynamic_slice_in_dim(query_code, block_index * BLOCK, BLOCK, 0)
        scale_row = lax.dynamic_slice_in_dim(column_scale, block_index, 1, 0)
        product = jnp.dot(code_block, weight_block, preferred_element_type=jnp.float32)
        return running + product * scale_row

    running = lax.fori_loop(
        0,
        block_total,
        add_block,
        jnp.zeros((own_rows * lax.axis_size("row"), out_width), jnp.float32),
    )
    query_proj = lax.psum_scatter(
        running * scale_rows[:, None], "row", scatter_dimension=0, tiled=True
    ).astype(jnp.bfloat16)
    return (query_proj, query_code, query_scale, keyval_code, keyval_scale)


def solution(mesh):
    in_specs = (P("col", "row"), P("row", "col"), P("row", "col"))
    out_specs = (
        P("row", "col"),
        P("row", "col"),
        P("row", "col"),
        P("row", "col"),
        P("row", "col"),
    )
    return jax.shard_map(body, mesh=mesh, in_specs=in_specs, out_specs=out_specs, check_vma=False)
```

profile of v0, /device:TPU:2, one launch (start us, length us, event | category | flops | bytes accessed | tf_op | source)
XLA Modules:
  0.0 286.5 jit_solution(13215520289935664740)
XLA Ops:
  7.2 1.3 abs_reduce_fusion
  8.5 1.0 abs_reduce_fusion.2
  9.6 41.3 %all-reduce.1 = (f32[512]{0:T(512)S(1)}, f32[512]{0:T(512)S(1)}) all-reduce(f32[512]{0:T(512)S(1)} %maximum_convert_fusion, bf16[512]{0:T(512)(128)(2,1)S(1)} %abs_reduce_fusion.3), channel_id=1, replica_groups=mesh['row'=32,'col'=16] {'col'}, use_global_device_ids=true, to_apply=%region_4.0 | all-reduce | flops 1024 | bytes 7168 | tf_op jit(solution)/shard_map/pmax | solution.py:40
  51.2 1.3 abs.29
  52.6 1.5 reduce_max.65
  54.2 0.5 copy-done.4
  54.9 4.0 %subtract_convert_fusion = bf16[512,512]{1,0:T(8,128)(2,1)S(1)} fusion(f32[64,8,4,128]{3,2,1,0:T(4,128)S(1)} %bitcast.21, bf16[512,512]{1,0:T(8,128)(2,1)S(1)} %copy-done, f32[512]{0:T(512)S(1)} %fusion.7), kind=kLoop, calls=%fused_computation.7 | loop fusion | flops 1835008 | bytes 2099200 | tf_op jit(solution)/shard_map/convert_element_type | solution.py:24
  58.9 47.3 %pmax.23 = f32[32]{0:T(128)S(1)} all-reduce(f32[32]{0:T(128)S(1)} %fusion.6), channel_id=1, replica_groups=mesh['row'=32,'col'=16] {'row'}, use_global_device_ids=true, to_apply=%region_6.0 | all-reduce | flops 32 | bytes 256 | tf_op jit(solution)/shard_map/pmax | solution.py:45
  106.2 0.3 subtract_convert_fusion.2
  106.6 25.4 %all_gather.6 = bf16[512,512]{1,0:T(8,128)(2,1)S(1)} all-gather(bf16[32,512]{1,0:T(8,128)(2,1)S(1)} %subtract_convert_fusion.2), channel_id=1, replica_groups=mesh['row'=32,'col'=16] {'col'}, dimensions={0}, use_global_device_ids=true | all-gather | bytes 557056 | tf_op jit(solution)/shard_map/all_gather | solution.py:48
  132.0 1.9 while.14
  132.0 0.4 fusion.15
  132.5 0.4 fusion.15
  133.0 0.4 fusion.15
  133.5 0.4 fusion.15
  133.9 1.3 dynamic-slice
  135.9 0.2 dynamic-update-slice
  136.1 35.7 %all-reduce = bf16[512]{0:T(512)(128)(2,1)S(1)} all-reduce(bf16[512]{0:T(512)(128)(2,1)S(1)} %dynamic-update-slice), channel_id=1, replica_groups=mesh['row'=32,'col'=16] {'col'}, use_global_device_ids=true, to_apply=%add | all-reduce | flops 512 | bytes 2048
  171.9 1.1 broadcast_multiply_fusion
  173.0 0.9 copy-done.2
  174.2 0.5 fusion.9
  174.8 1.7 subtract_convert_fusion.1
  176.5 101.8 %reduce-scatter.2.cloned.1.call-done = f32[16,512]{1,0:T(8,128)} async-done(((f32[512,512]{1,0:T(8,128)}), f32[16,512]{1,0:T(8,128)}) %reduce-scatter.2.cloned.1.call-update) | async-done | bytes 32784 | tf_op jit(solution)/shard_map/reduce_scatter | solution.py:70
  278.3 1.4 convert_element_type.45
  (30 shorter events, 1.2 us)
Async XLA Ops:
  7.2 43.8 %copy-start = (bf16[512,512]{1,0:T(8,128)(2,1)S(1)}, bf16[512,512]{1,0:T(8,128)(2,1)}, u32[]{:S(2)}) copy-start(bf16[512,512]{1,0:T(8,128)(2,1)} %param.6) | copy-start | bytes 1572868
  7.2 271.1 %reduce-scatter.2.cloned.1.call-start = ((), (), s32[]{:S(2)}) async-start(), calls=%async_computation.1 | async-start | bytes 1081344 | tf_op jit(solution)/shard_map/reduce_scatter | solution.py:70
  8.5 1.0 copy-start.3
  54.1 0.6 copy-start.4
  133.9 39.1 %copy-start.1 = (bf16[512,512]{1,0:T(8,128)(2,1)}, bf16[512,512]{1,0:T(8,128)(2,1)S(1)}, u32[]{:S(2)}) copy-start(bf16[512,512]{1,0:T(8,128)(2,1)S(1)} %get-tuple-element.195) | copy-start | bytes 1572868
  173.0 0.9 copy-start.2
Sparse Core Ops, SparseCore 0:
  173.1 105.1 reduce-scatter.1
where the time goes:
time: 287 us
  blocking collectives  150 us (52%)
  waiting for transfers between devices  102 us (36%)
  between operations  14.8 us (5%)
  other arithmetic  13.5 us (5%)
  local copies, waits for them, and re-layouts  4.68 us (2%)
    reduce_scatter x1, waiting for transfers between devices, body(): lax.psum_scatter(running * scale_rows[:, None], 'row', scatter_dimension=...  102 us
    pmax x1, blocking collectives, body(): row_peak = lax.pmax(jnp.max(jnp.abs(x_smooth), axis=1), 'row')  47.3 us
    pmax x1, blocking collectives, body(): act_peak, weight_peak = lax.pmax((act_local, weight_local), 'col')  41.3 us
    unnamed x1, blocking collectives  35.7 us
    all_gather x1, blocking collectives, body(): lax.all_gather(local_code, 'col', axis=0, tiled=True)  25.4 us
  transfers between devices with their start and end apart: 1, of which 1 were waited for; matrix products, arithmetic and copies ran while one was open for 1% of the time, Pallas kernels for 0%

commit v1 on v0

--- a/solution.py
+++ b/solution.py
@@ -45,7 +45,9 @@
     row_peak = lax.pmax(jnp.max(jnp.abs(x_smooth), axis=1), "row")
     local_code, local_scale = token_encode(x_smooth, row_peak)
     x_code, token_scale = (
-        lax.all_gather(local_code, "col", axis=0, tiled=True),
+        jnp.concatenate(
+            lax.all_to_all(jnp.stack([local_code] * lax.axis_size("col")), "col", 0, 0), axis=0
+        ),
         lax.all_gather(local_scale, "col", axis=0, tiled=True),
     )
     column_scale = jnp.repeat(query_scale, BLOCK, axis=1)

time: 287 us -> 272 us (0.948)
  blocking collectives: 150 us -> 125 us
  starting transfers between devices: 0.04 us -> 8.05 us
  waiting for transfers between devices: 102 us -> 105 us
    all_gather x1 -> x0, blocking collectives: 25.4 us -> none  [body(): lax.all_gather(local_code, 'col', axis=0, tiled=True)]
    all_to_all x0 -> x1, starting transfers between devices: none -> 8.01 us  [body(): lax.all_to_all(jnp.stack([local_code] * lax.axis_size('col')), 'col', 0, 0)]
  transfers between devices with their start and end apart: 1 -> 2, of which waited for: 1 -> 1; matrix products, arithmetic and copies ran while one was open for 1% -> 4% of each run, Pallas kernels for 0% -> 0%
where the time goes in v1:
time: 272 us
  blocking collectives  125 us (46%)
  waiting for transfers between devices  105 us (39%)
  between operations  14.8 us (5%)
  other arithmetic  12.6 us (5%)
  starting transfers between devices  8.05 us (3%)
  local copies, waits for them, and re-layouts  4.72 us (2%)
    reduce_scatter x1, waiting for transfers between devices, body(): lax.psum_scatter(running * scale_rows[:, None], 'row', scatter_dimension=...  105 us
    pmax x1, blocking collectives, body(): row_peak = lax.pmax(jnp.max(jnp.abs(x_smooth), axis=1), 'row')  47.3 us
    pmax x1, blocking collectives, body(): act_peak, weight_peak = lax.pmax((act_local, weight_local), 'col')  41.3 us
    unnamed x1, blocking collectives  36.4 us
    all_to_all x1, starting transfers between devices, body(): lax.all_to_all(jnp.stack([local_code] * lax.axis_size('col')), 'col', 0, 0)  8.01 us
    convert_element_type x2, other arithmetic, block_codes(): soften(tile_view / scales[:, None, :, None]).reshape(height, breadth)  5.69 us
  transfers between devices with their start and end apart: 2, of which 1 were waited for; matrix products, arithmetic and copies ran while one was open for 4% of the time, Pallas kernels for 0%

profile of v1, /device:TPU:2, one launch (start us, length us, event | category | flops | bytes accessed | tf_op | source)
XLA Modules:
  0.0 271.8 jit_solution(5406216888413707734)
XLA Ops:
  7.2 1.3 abs_reduce_fusion
  8.6 0.6 copy-done.3
  9.2 41.3 %all-reduce.1 = (f32[512]{0:T(512)S(1)}, f32[512]{0:T(512)S(1)}) all-reduce(f32[512]{0:T(512)S(1)} %maximum_convert_fusion, bf16[512]{0:T(512)(128)(2,1)S(1)} %abs_reduce_fusion.3), channel_id=1, replica_groups=mesh['row'=32,'col'=16] {'col'}, use_global_device_ids=true, to_apply=%region_4.0 | all-reduce | flops 1024 | bytes 7168 | tf_op jit(solution)/shard_map/pmax | solution.py:40
  50.7 47.3 %pmax.23 = f32[32]{0:T(128)S(1)} all-reduce(f32[32]{0:T(128)S(1)} %fusion.6), channel_id=1, replica_groups=mesh['row'=32,'col'=16] {'row'}, use_global_device_ids=true, to_apply=%region_6.0 | all-reduce | flops 32 | bytes 256 | tf_op jit(solution)/shard_map/pmax | solution.py:45
  98.0 0.3 subtract_convert_fusion.2
  98.4 0.8 stack.2
  99.2 8.0 %all-to-all-start = ((bf16[16,32,512]{2,1,0:T(8,128)(2,1)}), bf16[16,32,512]{2,1,0:T(8,128)(2,1)S(1)}, u32[]{:S(2)}, u32[]{:S(2)}) async-start(bf16[16,32,512]{2,1,0:T(8,128)(2,1)} %stack.2), calls=%async_computation | async-start | bytes 1048576 | tf_op jit(solution)/shard_map/all_to_all | solution.py:49
  107.5 1.3 abs.29
  108.8 1.5 reduce_max.65
  110.4 1.3 dynamic-slice
  112.3 0.2 dynamic-update-slice
  112.6 36.4 %all-reduce = bf16[512]{0:T(512)(128)(2,1)S(1)} all-reduce(bf16[512]{0:T(512)(128)(2,1)S(1)} %dynamic-update-slice), channel_id=1, replica_groups=mesh['row'=32,'col'=16] {'col'}, use_global_device_ids=true, to_apply=%add | all-reduce | flops 512 | bytes 2048
  149.2 4.0 %subtract_convert_fusion = bf16[512,512]{1,0:T(8,128)(2,1)S(1)} fusion(f32[64,8,4,128]{3,2,1,0:T(4,128)S(1)} %bitcast.22, bf16[512,512]{1,0:T(8,128)(2,1)S(1)} %copy-done, f32[512]{0:T(512)S(1)} %fusion.7), kind=kLoop, calls=%fused_computation.7 | loop fusion | flops 1835008 | bytes 2099200 | tf_op jit(solution)/shard_map/convert_element_type | solution.py:24
  153.2 1.9 while.14
  153.3 0.4 fusion.15
  153.8 0.4 fusion.15
  154.2 0.4 fusion.15
  154.7 0.4 fusion.15
  155.2 1.2 broadcast_multiply_fusion
  156.3 0.2 abs_reduce_fusion.1
  156.7 0.5 fusion.9
  157.3 1.7 subtract_convert_fusion.1
  158.9 104.6 %reduce-scatter.2.cloned.1.call-done = f32[16,512]{1,0:T(8,128)} async-done(((f32[512,512]{1,0:T(8,128)}), f32[16,512]{1,0:T(8,128)}) %reduce-scatter.2.cloned.1.call-update) | async-done | bytes 32784 | tf_op jit(solution)/shard_map/reduce_scatter | solution.py:72
  263.6 1.4 convert_element_type.45
  (32 shorter events, 1.1 us)
Async XLA Ops:
  7.2 1.3 copy-start.2
  8.4 0.8 copy-start.3
  99.2 8.1 %copy-start = (bf16[512,512]{1,0:T(8,128)(2,1)S(1)}, bf16[512,512]{1,0:T(8,128)(2,1)}, u32[]{:S(2)}) copy-start(bf16[512,512]{1,0:T(8,128)(2,1)} %param.6) | copy-start | bytes 1572868
  99.2 54.0 %all-to-all-start = ((bf16[16,32,512]{2,1,0:T(8,128)(2,1)}), bf16[16,32,512]{2,1,0:T(8,128)(2,1)S(1)}, u32[]{:S(2)}, u32[]{:S(2)}) async-start(bf16[16,32,512]{2,1,0:T(8,128)(2,1)} %stack.2), calls=%async_computation | async-start | bytes 1048576 | tf_op jit(solution)/shard_map/all_to_all | solution.py:49
  107.2 156.3 %reduce-scatter.2.cloned.1.call-start = ((), (), s32[]{:S(2)}) async-start(), calls=%async_computation.2 | async-start | bytes 1081344 | tf_op jit(solution)/shard_map/reduce_scatter | solution.py:72
  110.3 38.7 %copy-start.4 = (f32[4,4]{1,0:T(4,128)}, f32[4,4]{1,0:T(4,128)S(1)}, u32[]{:S(2)}) copy-start(f32[4,4]{1,0:T(4,128)S(1)} %add_multiply_fusion) | copy-start | bytes 196
  155.1 1.2 copy-start.1
Sparse Core Ops, SparseCore 0:
  156.5 107.0 reduce-scatter.1
